TPU v7x, 32 devices: a whole 2x2x4 slice. The times are simulated.
32 devices in a mesh: visit: 2 (over core), tx: 4 (over y, x), ty: 4 (over z).
Axes of the slice: x: 2, y: 2, z: 4, core: 2. Of those that a mesh axis runs over, the one named last changes fastest.
Arguments:
- raw: bfloat16 [4, 2048, 2048], P('visit', ('tx', 'ty')), may hold values from -12 to 12, as said below
- dark: float32 [2048, 2048], P(('tx', 'ty')), may hold values from 0 to 0.8
- flat: float32 [2048, 2048], P(('tx', 'ty')), may hold values from 0.5 to 1.5
- mask: int32 [4, 2048, 2048], P('visit', ('tx', 'ty')), may hold values 0 or 1
- offsets: int32 [4, 2], P('visit'), may hold values from 0 to 255
- scales: float32 [4, 2], P('visit'), may hold values from 0.985 to 1.015
- fracs: float32 [4, 2], P('visit'), may hold values from 0 to 1
Outputs:
- coadd: float32 [2048, 2048], P('visit', ('tx', 'ty'))
Inputs may be any that keep to these rules, and one draw needn't show every extreme that they name: `raw`: each exposure's pixels have a noise level of its own.
All inputs are finite; a program needn't handle non-finite values. No bound on the sum of `mask` on one device may be relied on, other than what follows from the above.
Results may differ from a plain program's by a relative error of at most 0.00145.
The roundings to bfloat16 on the way count: a program that leaves them out, or rounds other values in their place, can miss the bound.
Values may be sent and summed in bfloat16 or wider, within the bound.
A program may use at most 64 MiB of HBM per device.

v0:
```python
import functools

import jax
import jax.numpy as jnp
from jax import lax
from jax.experimental import pallas as pl
from jax.experimental.pallas import tpu as pltpu
from jax.sharding import PartitionSpec as P

MESH = pl.DeviceIdType.MESH
COL_WINDOW = 640
COL_ALIGN = 128
ROW_WINDOW = 512
ROW_ALIGN = 64


def sinc(t):
    at = jnp.pi * jnp.where(t == 0.0, 1.0, t)
    return jnp.where(t == 0.0, 1.0, jnp.sin(at) / at)


def lanczos(t):
    return jnp.where(jnp.abs(t) < 3.0, sinc(t) * sinc(t / 3.0), 0.0)


def banded(taps, first, window):
    frame = (lax.broadcasted_iota(jnp.int32, (window, taps.shape[1]), 0) + first).astype(jnp.float32)
    step = frame - taps[6:7, :]
    total = jnp.zeros_like(step)
    for tap in range(6):
        total = jnp.where(step == float(tap - 2), taps[tap : tap + 1, :], total)
    return total.astype(jnp.bfloat16)


def window_start(sky, frame_len, window, align):
    lowest = lax.div(lax.max((sky - 255) * 197 - 800, 0), 200)
    return pl.multiple_of(lax.min(lax.div(lowest, align) * align, frame_len - window), align)


def kernel(dims, offsets, scales, fracs, raw_in, dark_in, flat_in, mask_in, out, *scratch):
    exposures, parts, band, frame_len, visits, n_tx, n_ty = dims
    raw, dark, flat, mask, taps, rowk, image, outgoing, stats, totals, partial = scratch[:11]
    strips = scratch[11 : 11 + exposures]
    in_sem, send_sem, recv_sem, stat_send, stat_recv, sum_send, sum_recv = scratch[11 + exposures :]
    width = frame_len // parts
    vi, ti, yi = lax.axis_index("visit"), lax.axis_index("tx"), lax.axis_index("ty")
    me = ti * n_ty + yi

    half = n_ty // 2
    own_step = parts - 1

    def peer(step):
        high, at = 1 - lax.div(step, parts // 2), lax.rem(step, parts // 2)
        low, over = lax.rem(lax.div(at, n_tx) + 1, half), lax.rem(lax.rem(at, n_tx) + 1, n_tx)
        to_y = lax.rem(lax.div(yi, half) + high, 2) * half + lax.rem(lax.rem(yi, half) + low, half)
        to_t = lax.rem(ti + over, n_tx)
        return to_t * n_ty + to_y, (vi, to_t, to_y)

    loads = [(dark_in, dark), (flat_in, flat)]
    for expo in range(exposures):
        loads += [(raw_in.at[expo], raw.at[expo]), (mask_in.at[expo], mask.at[expo])]
    loads = [pltpu.make_async_copy(src, dst, in_sem.at[n]) for n, (src, dst) in enumerate(loads)]
    for load in loads:
        load.start()

    barrier = pltpu.get_barrier_semaphore()

    def greet(step, carry):
        pl.semaphore_signal(barrier, inc=1, device_id=peer(step)[1], device_id_type=MESH)
        return carry

    def greet_visit(step, carry):
        to = (lax.rem(vi + step, visits), ti, yi)
        pl.semaphore_signal(barrier, inc=1, device_id=to, device_id_type=MESH)
        return carry

    lax.fori_loop(0, own_step, greet, 0)
    lax.fori_loop(1, visits, greet_visit, 0)

    def weigh(expo, axis):
        shape = (8, frame_len)
        sky = lax.broadcasted_iota(jnp.int32, shape, 1).astype(jnp.float32)
        tap = lax.broadcasted_iota(jnp.int32, shape, 0).astype(jnp.float32)
        offset = offsets[expo, axis].astype(jnp.float32)
        coords = (sky - offset) * scales[expo, axis] + fracs[expo, axis]
        base = jnp.floor(coords)
        values = lanczos(coords - (base + (tap - 2.0)))
        taps[expo, axis, :, :] = jnp.where(tap < 6.0, values, base)

    def correct(expo):
        def chunk(at, carry):
            sumsq, count = carry
            cols = pl.ds(pl.multiple_of(at * 128, 128), 128)
            good = mask[expo, :, cols].astype(jnp.float32)
            fixed = (raw[expo, :, cols].astype(jnp.float32) - dark[:, cols]) * flat[:, cols] * good
            image[expo, 0:band, cols] = fixed.astype(jnp.bfloat16)
            image[expo, band : 2 * band, cols] = good.astype(jnp.bfloat16)
            sumsq = sumsq + jnp.sum(fixed * fixed, axis=0, keepdims=True)
            count = count + jnp.sum(good, axis=0, keepdims=True)
            return sumsq, count

        zero = jnp.zeros((1, 128), jnp.float32)
        sumsq, count = lax.fori_loop(0, frame_len // 128, chunk, (zero, zero))
        stats[me, expo : expo + 1, :] = sumsq
        stats[me, exposures + expo : exposures + expo + 1, :] = count

    def strip_copy(expo, step):
        return pltpu.make_async_remote_copy(
            src_ref=outgoing.at[expo, step],
            dst_ref=strips[expo].at[pl.ds(pl.multiple_of(me * band, band), band), :],
            send_sem=send_sem.at[expo, step],
            recv_sem=recv_sem.at[expo, step],
            device_id=peer(step)[1],
            device_id_type=MESH,
        )

    def stat_copy(step):
        return pltpu.make_async_remote_copy(
            src_ref=stats.at[me],
            dst_ref=stats.at[me],
            send_sem=stat_send.at[step],
            recv_sem=stat_recv.at[step],
            device_id=peer(step)[1],
            device_id_type=MESH,
        )

    def column(expo, step):
        to, _ = peer(step)
        first = window_start(to * width, frame_len, COL_WINDOW, COL_ALIGN)
        cols = pl.ds(pl.multiple_of(to * width, width), width)
        k = banded(taps[expo, 1, :, cols], first, COL_WINDOW)
        operand = image[expo, :, pl.ds(first, COL_WINDOW)]
        return jnp.dot(operand, k, preferred_element_type=jnp.float32).astype(jnp.bfloat16)

    def send_stat(step, carry):
        stat_copy(step).start()
        return carry

    weigh(0, 1)
    loads[0].wait()
    loads[1].wait()
    for expo in range(exposures):
        if expo > 0:
            weigh(expo, 1)
        loads[2 + 2 * expo].wait()
        loads[3 + 2 * expo].wait()
        correct(expo)
        if expo == 0:
            pl.semaphore_wait(barrier, parts + visits - 2)
        if expo == exposures - 1:
            lax.fori_loop(0, own_step, send_stat, 0)

        def send_step(step, carry, expo=expo):
            step = lax.rem(step, 2) * (parts // 2) + lax.div(step, 2)
            both = column(expo, step)
            outgoing[expo, step, :, 0:width] = both[0:band]
            outgoing[expo, step, :, width : 2 * width] = both[band : 2 * band]
            strip_copy(expo, step).start()
            return carry

        lax.fori_loop(0, own_step, send_step, 0)
        both = column(expo, own_step)
        rows = pl.ds(pl.multiple_of(me * band, band), band)
        strips[expo][rows, 0:width] = both[0:band]
        strips[expo][rows, width : 2 * width] = both[band : 2 * band]

    for expo in range(exposures):
        weigh(expo, 0)

        def build(block, carry, expo=expo):
            at = pl.multiple_of(block * 128, 128)
            first = window_start(at, frame_len, ROW_WINDOW, ROW_ALIGN)
            rowk[expo, pl.ds(at, 128), :] = banded(taps[expo, 0, :, pl.ds(at, 128)], first, ROW_WINDOW).T
            return carry

        lax.fori_loop(0, frame_len // 128, build, 0)

    def wait_stat(step, carry):
        stat_copy(step).wait()
        return carry

    own = frame_len // visits
    blocks = own // 128

    def sum_copy(step, block):
        to = lax.rem(vi + step, visits)
        at = pl.multiple_of(to * own + block * 128, 128)
        return pltpu.make_async_remote_copy(
            src_ref=totals.at[pl.ds(at, 128), :],
            dst_ref=partial.at[step, pl.ds(pl.multiple_of(block * 128, 128), 128), :],
            send_sem=sum_send.at[step, block],
            recv_sem=sum_recv.at[step, block],
            device_id=(to, ti, yi),
            device_id_type=MESH,
        )

    for expo in range(exposures):

        def wait_strip(step, carry, expo=expo):
            strip_copy(expo, step).wait()
            return carry

        lax.fori_loop(0, own_step, wait_strip, 0)
        if expo == 0:
            lax.fori_loop(0, own_step, wait_stat, 0)
            lanes = jnp.sum(stats[...], axis=0)
            sums = jnp.sum(lanes, axis=1, keepdims=True)
        count = sums[exposures + expo : exposures + expo + 1, :]
        weight = count / (sums[expo : expo + 1, :] + 1e-05 * count)

        def row(at, expo=expo, weight=weight):
            at = pl.multiple_of(at, 128)
            first = window_start(at, frame_len, ROW_WINDOW, ROW_ALIGN)
            rows = pl.ds(at, 128)
            operand = strips[expo][pl.ds(first, ROW_WINDOW), :]
            k = rowk[expo, rows, :]
            warped = weight * jnp.dot(k, operand, preferred_element_type=jnp.float32)
            totals[rows, :] = warped if expo == 0 else totals[rows, :] + warped

        last = expo == exposures - 1

        def row_step(index, carry, row=row, last=last):
            step, block = lax.div(index, blocks) + 1, lax.rem(index, blocks)
            row(lax.rem(vi + step, visits) * own + block * 128)
            if last:
                sum_copy(step, block).start()
            return carry

        def own_row(block, carry, row=row):
            row(vi * own + block * 128)
            return carry

        lax.fori_loop(0, (visits - 1) * blocks, row_step, 0)
        lax.fori_loop(0, blocks, own_row, 0)

    def finish(block, carry):
        rows = pl.ds(pl.multiple_of(block * 128, 128), 128)
        total = totals[pl.ds(pl.multiple_of(vi * own + block * 128, 128), 128), :]
        for step in range(1, visits):
            sum_copy(step, block).wait()
            total = total + partial[step, rows, :]
        out[rows, :] = total[:, 0:width] / jnp.maximum(total[:, width : 2 * width], 1.0)
        return carry

    lax.fori_loop(0, blocks, finish, 0)


def shards(n_visit, n_tx, n_ty, raw, dark, flat, mask, offsets, scales, fracs):
    exposures, band, frame_len = raw.shape
    parts = n_tx * n_ty
    width = frame_len // parts
    own = frame_len // n_visit
    smem = pl.BlockSpec(memory_space=pltpu.SMEM)
    vmem = pl.BlockSpec(memory_space=pltpu.VMEM)
    dims = (exposures, parts, band, frame_len, n_visit, n_tx, n_ty)
    dma = pltpu.SemaphoreType.DMA
    return pl.pallas_call(
        functools.partial(kernel, dims),
        out_shape=jax.ShapeDtypeStruct((own, width), jnp.float32),
        in_specs=[smem] * 3 + [pl.BlockSpec(memory_space=pl.ANY)] * 4,
        out_specs=vmem,
        scratch_shapes=[
            pltpu.VMEM(raw.shape, raw.dtype),
            pltpu.VMEM(dark.shape, dark.dtype),
            pltpu.VMEM(flat.shape, flat.dtype),
            pltpu.VMEM(mask.shape, mask.dtype),
            pltpu.VMEM((exposures, 2, 8, frame_len), jnp.float32),
            pltpu.VMEM((exposures, frame_len, ROW_WINDOW), jnp.bfloat16),
            pltpu.VMEM((exposures, 2 * band, frame_len), jnp.bfloat16),
            pltpu.VMEM((exposures, parts, band, 2 * width), jnp.bfloat16),
            pltpu.VMEM((parts, 2 * exposures, 128), jnp.float32),
            pltpu.VMEM((frame_len, 2 * width), jnp.float32),
            pltpu.VMEM((n_visit, own, 2 * width), jnp.float32),
        ]
        + [pltpu.VMEM((frame_len, 2 * width), jnp.bfloat16)] * exposures
        + [
            dma((2 + 2 * exposures,)),
            dma((exposures, parts)),
            dma((exposures, parts)),
            dma((parts,)),
            dma((parts,)),
            dma((n_visit, own // 128)),
            dma((n_visit, own // 128)),
        ],
        compiler_params=pltpu.CompilerParams(
            collective_id=0, has_side_effects=True, vmem_limit_bytes=60000000
        ),
    )(offsets, scales, fracs, raw, dark, flat, mask)


def solution(mesh):
    in_specs = (
        P("visit", ("tx", "ty"), None),
        P(("tx", "ty"), None),
        P(("tx", "ty"), None),
        P("visit", ("tx", "ty"), None),
        P("visit", None),
        P("visit", None),
        P("visit", None),
    )
    out_specs = P("visit", ("tx", "ty"))
    body = functools.partial(shards, mesh.shape["visit"], mesh.shape["tx"], mesh.shape["ty"])
    return jax.shard_map(body, mesh=mesh, in_specs=in_specs, out_specs=out_specs, check_vma=False)
```

profile of v0, /device:TPU:0, one launch (start us, length us, event | category | flops | bytes accessed | tf_op | source)
XLA Modules:
  0.0 62.6 jit_solution(892859304589076653)
XLA Ops:
  0.0 60.8 %shard_map.73 = f32[1024,128]{1,0:T(8,128)} custom-call(s32[2,2]{1,0:T(2,128)} %offsets.1, f32[2,2]{1,0:T(2,128)} %scales.1, f32[2,2]{1,0:T(2,128)} %fracs.1, bf16[2,128,2048]{2,1,0:T(8,128)(2,1)} %raw_in.1, f32[128,2048]{1,0:T(8,128)} %dark_in.1, f32[128,2048]{1,0:T(8,128)} %flat_in.1, s32[2,128,2048]{2,1,0:T(8,128)} %mask_in.1), custom_call_target="tpu_custom_call" | custom-call | tf_op jit(solution)/shard_map/pallas_call | solution.py:257
  60.8 1.9 %copy.9 = f32[1024,128]{1,0:T(8,128)} copy(f32[1024,128]{1,0:T(8,128)} %shard_map.73) | data formatting | bytes 1048576
where the time goes:
time: 62.8 us; the launch traced here: 62.6 us
  Pallas kernels  60.8 us (97%)
  local copies, waits for them, and re-layouts  1.87 us (3%)
    pallas_call x1, Pallas kernels, shards(): pl.pallas_call(functools.partial(kernel, dims), out_shape=jax.ShapeDtypeS...  60.8 us
    unnamed x1, local copies, waits for them, and re-layouts  1.87 us

commit v1 on v0

v1 whole, which is shorter than its diff:
```python
import functools
import math

import jax
import jax.numpy as jnp
from jax import lax
from jax.experimental import pallas as pl
from jax.experimental.pallas import tpu as pltpu
from jax.sharding import PartitionSpec as P

MESH = pl.DeviceIdType.MESH
BLOCK = 128
COL_ALIGN = 128
ROW_ALIGN = 32
SINE = [(-1) ** n * math.pi ** (2 * n + 1) / math.factorial(2 * n + 1) for n in range(6)]


def window_size(frame_len, align):
    return min(frame_len, -(-(3 * frame_len // 100 + BLOCK + 267 + align) // 128) * 128)


def sin_pi(t):
    near = jnp.floor(t + 0.5)
    r = t - near
    r2 = r * r
    total = jnp.full_like(r, SINE[-1])
    for c in SINE[-2::-1]:
        total = total * r2 + c
    odd = near - 2.0 * jnp.floor(near * 0.5)
    return total * r * (1.0 - 2.0 * odd)


def lanczos(t):
    safe = jnp.where(jnp.abs(t) < 1e-4, 1.0, t)
    value = sin_pi(safe) * sin_pi(safe / 3.0) * (3.0 / math.pi**2) / (safe * safe)
    value = jnp.where(jnp.abs(t) < 1e-4, 1.0, value)
    return jnp.where(jnp.abs(t) < 3.0, value, 0.0)


def banded(taps, first, window):
    frame = (lax.broadcasted_iota(jnp.int32, (window, taps.shape[1]), 0) + first).astype(jnp.float32)
    step = frame - taps[6:7, :]
    total = jnp.zeros_like(step)
    for tap in range(6):
        total = jnp.where(step == float(tap - 2), taps[tap : tap + 1, :], total)
    return total.astype(jnp.bfloat16)


def window_start(sky, frame_len, window, align):
    lowest = lax.div(lax.max((sky - 255) * 197 - 800, 0), 200)
    return pl.multiple_of(lax.min(lax.div(lowest, align) * align, frame_len - window), align)


def kernel(dims, offsets, scales, fracs, raw_in, dark_in, flat_in, mask_in, out, *scratch):
    exposures, parts, band, frame_len, visits, n_tx, n_ty, relay = dims
    raw, dark, flat, mask, taps, rowk, image, outgoing, stats, totals, partial = scratch[:11]
    rest = list(scratch[11:])
    strips = [rest.pop(0) for _ in range(exposures)]
    in_sem, send_sem, recv_sem, stat_send, stat_recv, sum_send, sum_recv = [rest.pop(0) for _ in range(7)]
    if relay:
        auxs = [rest.pop(0) for _ in range(exposures)]
        fills = [rest.pop(0) for _ in range(exposures)]
        aux_totals, aux_partial, relay_out, relay_in = [rest.pop(0) for _ in range(4)]
        aux_recv, aux_send, aux_sum_recv, relay_send, relay_recv = [rest.pop(0) for _ in range(5)]
    width = frame_len // parts
    col_window, row_window = window_size(frame_len, COL_ALIGN), window_size(frame_len, ROW_ALIGN)
    vi, ti, yi = lax.axis_index("visit"), lax.axis_index("tx"), lax.axis_index("ty")
    me = ti * n_ty + yi
    own = frame_len // visits
    blocks = own // BLOCK

    if relay:
        high = lax.div(yi, 2)
        depth = high * (3 - yi) + (1 - high) * yi
        inner = depth == 1
        outer = depth == 0
        hub_y, far_y = 1 + high, 3 * (1 - high)
        far_strip = ti * n_ty + far_y

    loads = [(dark_in, dark), (flat_in, flat)]
    for expo in range(exposures):
        loads += [(raw_in.at[expo], raw.at[expo]), (mask_in.at[expo], mask.at[expo])]
    loads = [pltpu.make_async_copy(src, dst, in_sem.at[n]) for n, (src, dst) in enumerate(loads)]
    barrier = pltpu.get_barrier_semaphore()

    def peer(step):
        at = lax.rem(me + step, parts)
        return (vi, lax.div(at, n_ty), lax.rem(at, n_ty))

    def greet(step, carry):
        pl.semaphore_signal(barrier, inc=1, device_id=peer(step), device_id_type=MESH)
        return carry

    def greet_visit(step, carry):
        to = (lax.rem(vi + step, visits), ti, yi)
        pl.semaphore_signal(barrier, inc=1, device_id=to, device_id_type=MESH)
        return carry

    lax.fori_loop(1, parts, greet, 0)
    lax.fori_loop(1, visits, greet_visit, 0)
    for load in loads:
        load.start()

    def weigh(expo, axis):
        shape = (8, frame_len)
        sky = lax.broadcasted_iota(jnp.int32, shape, 1).astype(jnp.float32)
        tap = lax.broadcasted_iota(jnp.int32, shape, 0).astype(jnp.float32)
        offset = offsets[expo, axis].astype(jnp.float32)
        coords = (sky - offset) * scales[expo, axis] + fracs[expo, axis]
        base = jnp.floor(coords)
        values = lanczos(coords - (base + (tap - 2.0)))
        taps[expo, axis, :, :] = jnp.where(tap < 6.0, values, base)

    def correct(expo):
        def chunk(at, carry):
            sumsq, count = carry
            cols = pl.ds(pl.multiple_of(at * 128, 128), 128)
            good = mask[expo, :, cols].astype(jnp.float32)
            fixed = (raw[expo, :, cols].astype(jnp.float32) - dark[:, cols]) * flat[:, cols] * good
            image[expo, 0:band, cols] = fixed.astype(jnp.bfloat16)
            image[expo, band : 2 * band, cols] = good.astype(jnp.bfloat16)
            sumsq = sumsq + jnp.sum(fixed * fixed, axis=0, keepdims=True)
            count = count + jnp.sum(good, axis=0, keepdims=True)
            return sumsq, count

        zero = jnp.zeros((1, 128), jnp.float32)
        sumsq, count = lax.fori_loop(0, frame_len // 128, chunk, (zero, zero))
        stats[me, expo : expo + 1, :] = sumsq
        stats[me, exposures + expo : exposures + expo + 1, :] = count

    def band_rows(source):
        return pl.ds(pl.multiple_of(source * band, band), band)

    def strip_copy(expo, strip, source, to, via=False):
        return pltpu.make_async_remote_copy(
            src_ref=outgoing.at[expo, strip],
            dst_ref=(auxs if via else strips)[expo].at[band_rows(source), :],
            send_sem=send_sem.at[expo, strip],
            recv_sem=(aux_recv if via else recv_sem).at[expo, source],
            device_id=to,
            device_id_type=MESH,
        )

    def stat_copy(source, step):
        return pltpu.make_async_remote_copy(
            src_ref=stats.at[source],
            dst_ref=stats.at[source],
            send_sem=stat_send.at[step],
            recv_sem=stat_recv.at[source],
            device_id=peer(step),
            device_id_type=MESH,
        )

    def column_kernel(expo, strip):
        first = window_start(strip * width, frame_len, col_window, COL_ALIGN)
        cols = pl.ds(pl.multiple_of(strip * width, width), width)
        return first, banded(taps[expo, 1, :, cols], first, col_window)

    def column(expo, strip):
        first, k = column_kernel(expo, strip)
        operand = image[expo, :, pl.ds(first, col_window)]
        return jnp.dot(operand, k, preferred_element_type=jnp.float32).astype(jnp.bfloat16)

    def put(ref, both):
        ref[:, 0:width] = both[0:band]
        ref[:, width : 2 * width] = both[band : 2 * band]

    if relay:
        groups = [(0, 0, 1), (1, 0, 1), (0, 1, 3), (1, 1, 3)]

        def target(index, head):
            group, over = lax.div(index, n_tx), lax.rem(index, n_tx)
            if head:
                reach = group * 0 + 3
            else:
                reach = lax.select(inner, lax.rem(2 * group + 2, 4) - lax.div(group, 2), 2 - group)
            via = reach == 3
            to_t = lax.rem(ti + over, n_tx)
            strip_y = high * (3 - reach) + (1 - high) * reach
            to_y = lax.select(via, hub_y, strip_y)
            return to_t * n_ty + strip_y, (vi, to_t, to_y), via, (to_t == ti) & (to_y == yi)

        def prepare(expo, index, head):
            strip, to, via, mine = target(index, head)
            both = column(expo, strip)

            @pl.when(jnp.logical_not(mine))
            def _():
                put(outgoing.at[expo, strip], both)

            @pl.when(mine & via)
            def _():
                put(auxs[expo].at[band_rows(me), :], both)

            @pl.when(mine & jnp.logical_not(via))
            def _():
                put(strips[expo].at[band_rows(me), :], both)

        def dispatch(expo, index, head, start):
            strip, to, via, mine = target(index, head)

            @pl.when(jnp.logical_not(mine) & via)
            def _():
                copy = strip_copy(expo, strip, me, to, True)
                copy.start() if start else copy.wait_send()

            @pl.when(jnp.logical_not(mine) & jnp.logical_not(via))
            def _():
                copy = strip_copy(expo, strip, me, to, False)
                copy.start() if start else copy.wait_send()

    else:
        groups = [(expo, 1, n_ty) for expo in range(exposures)]

        def target(index, head):
            group, over = lax.div(index, n_tx), lax.rem(index, n_tx)
            to_t, to_y = lax.rem(ti + over, n_tx), lax.rem(yi + group, n_ty)
            return to_t * n_ty + to_y, (vi, to_t, to_y), (to_t == ti) & (to_y == yi)

        def prepare(expo, index, head):
            strip, to, mine = target(index, head)
            both = column(expo, strip)

            @pl.when(jnp.logical_not(mine))
            def _():
                put(outgoing.at[expo, strip], both)

            @pl.when(mine)
            def _():
                put(strips[expo].at[band_rows(me), :], both)

        def dispatch(expo, index, head, start):
            strip, to, mine = target(index, head)

            @pl.when(jnp.logical_not(mine))
            def _():
                copy = strip_copy(expo, strip, me, to)
                copy.start() if start else copy.wait_send()

    def over_group(group, *actions):
        expo, tail, length = group

        def step(index, carry):
            for action in actions:
                action(expo, index, tail == 0)
            return carry

        lax.fori_loop(0, length * n_tx, step, 0)

    def begin(expo, index, head):
        dispatch(expo, index, head, True)

    def finish_send(expo, index, head):
        dispatch(expo, index, head, False)

    for expo in range(exposures):
        weigh(expo, 1)
    loads[0].wait()
    loads[1].wait()
    for expo in range(exposures):
        loads[2 + 2 * expo].wait()
        loads[3 + 2 * expo].wait()
        correct(expo)
    if relay:
        over_group(groups[0], prepare)
    pl.semaphore_wait(barrier, parts + visits - 2)

    def send_stat(step, carry):
        stat_copy(me, step).start()
        return carry

    lax.fori_loop(1, parts, send_stat, 0)
    if relay:
        over_group(groups[0], begin)
    for group in groups[1 if relay else 0 :]:
        over_group(group, prepare, begin)

    for expo in range(exposures):
        weigh(expo, 0)

        def build(block, carry, expo=expo):
            at = pl.multiple_of(block * BLOCK, BLOCK)
            first = window_start(at, frame_len, row_window, ROW_ALIGN)
            rowk[expo, pl.ds(at, BLOCK), :] = banded(taps[expo, 0, :, pl.ds(at, BLOCK)], first, row_window).T
            return carry

        lax.fori_loop(0, frame_len // BLOCK, build, 0)

    def wait_stat(step, carry):
        stat_copy(lax.rem(me + step, parts), step).wait()
        return carry

    lax.fori_loop(1, parts, wait_stat, 0)
    sums = jnp.sum(jnp.sum(stats[...], axis=0), axis=1, keepdims=True)
    weights, full = [], []
    for expo in range(exposures):
        count = sums[exposures + expo : exposures + expo + 1, :]
        weights.append(count / (sums[expo : expo + 1, :] + 1e-05 * count))
        full.append(jnp.where(2.0 * count >= float(frame_len * frame_len), 1.0, 0.0))

    def warp(expo, at, source):
        first = window_start(at, frame_len, row_window, ROW_ALIGN)
        return jnp.dot(
            rowk[expo, pl.ds(at, BLOCK), :],
            source[pl.ds(first, row_window), :],
            preferred_element_type=jnp.float32,
        )

    def block_rows(block):
        return pl.ds(pl.multiple_of(block * BLOCK, BLOCK), BLOCK)

    if relay:
        half_rows = 2 * band
        fill_strip = lax.select(inner, far_strip, me)

        def half_at(index, side):
            return pl.ds(pl.multiple_of(index * n_ty * band + side * half_rows, half_rows), half_rows)

        for expo in range(exposures):
            _, k = column_kernel(expo, fill_strip)
            cover = jnp.sum(k.astype(jnp.float32), axis=0, keepdims=True).astype(jnp.bfloat16)
            cover = cover.astype(jnp.float32) * full[expo]
            cover = jnp.broadcast_to(cover, (half_rows, width)).astype(jnp.bfloat16)
            blank = jnp.zeros((half_rows, width), jnp.bfloat16)

            @pl.when(inner)
            def _(expo=expo, cover=cover, blank=blank):
                for index in range(n_tx):
                    auxs[expo][half_at(index, 1 - high), 0:width] = blank
                    auxs[expo][half_at(index, 1 - high), width : 2 * width] = blank
                    fills[expo][half_at(index, 1 - high), :] = blank
                    fills[expo][half_at(index, high), :] = cover

            @pl.when(outer)
            def _(expo=expo, cover=cover, blank=blank):
                for index in range(n_tx):
                    strips[expo][half_at(index, 1 - high), 0:width] = blank
                    strips[expo][half_at(index, 1 - high), width : 2 * width] = cover

        def half_band(index):
            return lax.div(index, 2) * n_ty + high * 2 + lax.rem(index, 2)

        def aux_sum_copy(block):
            at = pl.multiple_of((1 - vi) * own + block * BLOCK, BLOCK)
            return pltpu.make_async_remote_copy(
                src_ref=aux_totals.at[pl.ds(at, BLOCK), :],
                dst_ref=aux_partial.at[block_rows(block), :],
                send_sem=aux_send.at[block],
                recv_sem=aux_sum_recv.at[block],
                device_id=(1 - vi, ti, yi),
                device_id_type=MESH,
            )

        def relay_copy(block):
            return pltpu.make_async_remote_copy(
                src_ref=relay_out.at[block_rows(block), :],
                dst_ref=relay_in.at[block_rows(block), :],
                send_sem=relay_send.at[block],
                recv_sem=relay_recv.at[block],
                device_id=(vi, ti, far_y),
                device_id_type=MESH,
            )

        def aux_row(at):
            at = pl.multiple_of(at, BLOCK)
            value = cover = 0.0
            for expo in range(exposures):
                both = warp(expo, at, auxs[expo])
                value = value + weights[expo] * both[:, 0:width]
                cover = cover + weights[expo] * (both[:, width : 2 * width] - warp(expo, at, fills[expo]))
            aux_totals[pl.ds(at, BLOCK), 0:width] = value
            aux_totals[pl.ds(at, BLOCK), width : 2 * width] = cover

        @pl.when(inner)
        def _():
            for expo in range(exposures):

                def wait_aux(index, carry, expo=expo):
                    source = half_band(index)

                    @pl.when(source != me)
                    def _():
                        strip_copy(expo, 0, source, (vi, ti, yi), True).wait_recv()

                    return carry

                lax.fori_loop(0, parts // 2, wait_aux, 0)

            def other_half(block, carry):
                aux_row((1 - vi) * own + block * BLOCK)
                aux_sum_copy(block).start()
                return carry

            def own_half(block, carry):
                at = pl.multiple_of(vi * own + block * BLOCK, BLOCK)
                aux_row(at)
                aux_sum_copy(block).wait()
                total = aux_totals[pl.ds(at, BLOCK), :] + aux_partial[block_rows(block), :]
                relay_out[block_rows(block), :] = total.astype(jnp.bfloat16)
                relay_copy(block).start()
                return carry

            lax.fori_loop(0, blocks, other_half, 0)
            lax.fori_loop(0, blocks, own_half, 0)

    def sum_copy(step, block):
        to = lax.rem(vi + step, visits)
        at = pl.multiple_of(to * own + block * BLOCK, BLOCK)
        return pltpu.make_async_remote_copy(
            src_ref=totals.at[pl.ds(at, BLOCK), :],
            dst_ref=partial.at[step, block_rows(block), :],
            send_sem=sum_send.at[step, block],
            recv_sem=sum_recv.at[step, block],
            device_id=(to, ti, yi),
            device_id_type=MESH,
        )

    for expo in range(exposures):

        def wait_strip(step, carry, expo=expo):
            source = lax.rem(me + step, parts)
            if relay:

                @pl.when(inner | (lax.div(lax.rem(source, n_ty), 2) == high))
                def _():
                    strip_copy(expo, 0, source, (vi, ti, yi)).wait_recv()

            else:
                strip_copy(expo, 0, source, (vi, ti, yi)).wait_recv()
            return carry

        lax.fori_loop(1, parts, wait_strip, 0)
        last = expo == exposures - 1

        def row(at, expo=expo):
            at = pl.multiple_of(at, BLOCK)
            warped = weights[expo] * warp(expo, at, strips[expo])
            rows = pl.ds(at, BLOCK)
            totals[rows, :] = warped if expo == 0 else totals[rows, :] + warped

        def row_step(index, carry, row=row, last=last):
            step, block = lax.div(index, blocks) + 1, lax.rem(index, blocks)
            row(lax.rem(vi + step, visits) * own + block * BLOCK)
            if last:
                sum_copy(step, block).start()
            return carry

        def own_row(block, carry, row=row):
            row(vi * own + block * BLOCK)
            return carry

        lax.fori_loop(0, (visits - 1) * blocks, row_step, 0)
        lax.fori_loop(0, blocks, own_row, 0)

    def finish(block, carry):
        total = totals[pl.ds(pl.multiple_of(vi * own + block * BLOCK, BLOCK), BLOCK), :]
        for step in range(1, visits):
            sum_copy(step, block).wait()
            total = total + partial[step, block_rows(block), :]
        if relay:
            totals[pl.ds(pl.multiple_of(vi * own + block * BLOCK, BLOCK), BLOCK), :] = total

            @pl.when(outer)
            def _():
                relay_copy(block).wait_recv()
                at = pl.ds(pl.multiple_of(vi * own + block * BLOCK, BLOCK), BLOCK)
                totals[at, :] = total + relay_in[block_rows(block), :].astype(jnp.float32)

            total = totals[pl.ds(pl.multiple_of(vi * own + block * BLOCK, BLOCK), BLOCK), :]
        out[block_rows(block), :] = total[:, 0:width] / jnp.maximum(total[:, width : 2 * width], 1.0)
        return carry

    lax.fori_loop(0, blocks, finish, 0)

    for group in groups:
        over_group(group, finish_send)
    if relay:

        @pl.when(inner)
        def _():
            def sent(block, carry):
                relay_copy(block).wait_send()
                return carry

            lax.fori_loop(0, blocks, sent, 0)


def shards(n_visit, n_tx, n_ty, raw, dark, flat, mask, offsets, scales, fracs):
    exposures, band, frame_len = raw.shape
    parts = n_tx * n_ty
    width = frame_len // parts
    own = frame_len // n_visit
    blocks = own // BLOCK
    relay = n_visit == 2 and n_ty == 4 and exposures == 2
    row_window = window_size(frame_len, ROW_ALIGN)
    smem = pl.BlockSpec(memory_space=pltpu.SMEM)
    vmem = pl.BlockSpec(memory_space=pltpu.VMEM)
    dims = (exposures, parts, band, frame_len, n_visit, n_tx, n_ty, relay)
    dma = pltpu.SemaphoreType.DMA
    scratch = [
        pltpu.VMEM(raw.shape, raw.dtype),
        pltpu.VMEM(dark.shape, dark.dtype),
        pltpu.VMEM(flat.shape, flat.dtype),
        pltpu.VMEM(mask.shape, mask.dtype),
        pltpu.VMEM((exposures, 2, 8, frame_len), jnp.float32),
        pltpu.VMEM((exposures, frame_len, row_window), jnp.bfloat16),
        pltpu.VMEM((exposures, 2 * band, frame_len), jnp.bfloat16),
        pltpu.VMEM((exposures, parts, band, 2 * width), jnp.bfloat16),
        pltpu.VMEM((parts, 2 * exposures, 128), jnp.float32),
        pltpu.VMEM((frame_len, 2 * width), jnp.float32),
        pltpu.VMEM((n_visit, own, 2 * width), jnp.float32),
    ]
    scratch += [pltpu.VMEM((frame_len, 2 * width), jnp.bfloat16)] * exposures
    scratch += [
        dma((2 + 2 * exposures,)),
        dma((exposures, parts)),
        dma((exposures, parts)),
        dma((parts,)),
        dma((parts,)),
        dma((n_visit, blocks)),
        dma((n_visit, blocks)),
    ]
    if relay:
        scratch += [pltpu.VMEM((frame_len, 2 * width), jnp.bfloat16)] * exposures
        scratch += [pltpu.VMEM((frame_len, width), jnp.bfloat16)] * exposures
        scratch += [
            pltpu.VMEM((frame_len, 2 * width), jnp.float32),
            pltpu.VMEM((own, 2 * width), jnp.float32),
            pltpu.VMEM((own, 2 * width), jnp.bfloat16),
            pltpu.VMEM((own, 2 * width), jnp.bfloat16),
            dma((exposures, parts)),
            dma((blocks,)),
            dma((blocks,)),
            dma((blocks,)),
            dma((blocks,)),
        ]
    return pl.pallas_call(
        functools.partial(kernel, dims),
        out_shape=jax.ShapeDtypeStruct((own, width), jnp.float32),
        in_specs=[smem] * 3 + [pl.BlockSpec(memory_space=pl.ANY)] * 4,
        out_specs=vmem,
        scratch_shapes=scratch,
        compiler_params=pltpu.CompilerParams(
            collective_id=0, has_side_effects=True, vmem_limit_bytes=60000000
        ),
    )(offsets, scales, fracs, raw, dark, flat, mask)


def solution(mesh):
    in_specs = (
        P("visit", ("tx", "ty"), None),
        P(("tx", "ty"), None),
        P(("tx", "ty"), None),
        P("visit", ("tx", "ty"), None),
        P("visit", None),
        P("visit", None),
        P("visit", None),
    )
    out_specs = P("visit", ("tx", "ty"))
    body = functools.partial(shards, mesh.shape["visit"], mesh.shape["tx"], mesh.shape["ty"])
    return jax.shard_map(body, mesh=mesh, in_specs=in_specs, out_specs=out_specs, check_vma=False)
```

time: 62.8 us -> 57.9 us (0.922)
  Pallas kernels: 60.8 us -> 55.8 us
    pallas_call x1, Pallas kernels: 60.8 us -> 55.8 us  [shards(): pl.pallas_call(functools.partial(kernel, dims), out_shape=jax.ShapeDtypeS...]
where the time goes in v1:
time: 57.9 us; the launch traced here: 57.7 us
  Pallas kernels  55.8 us (96%)
  local copies, waits for them, and re-layouts  1.87 us (3%)
    pallas_call x1, Pallas kernels, shards(): pl.pallas_call(functools.partial(kernel, dims), out_shape=jax.ShapeDtypeS...  55.8 us
    unnamed x1, local copies, waits for them, and re-layouts  1.87 us

profile of v1, /device:TPU:0, one launch (start us, length us, event | category | flops | bytes accessed | tf_op | source)
XLA Modules:
  0.0 57.7 jit_solution(2402485288398653686)
XLA Ops:
  0.0 55.8 %shard_map.73 = f32[1024,128]{1,0:T(8,128)} custom-call(s32[2,2]{1,0:T(2,128)} %offsets.1, f32[2,2]{1,0:T(2,128)} %scales.1, f32[2,2]{1,0:T(2,128)} %fracs.1, bf16[2,128,2048]{2,1,0:T(8,128)(2,1)} %raw_in.1, f32[128,2048]{1,0:T(8,128)} %dark_in.1, f32[128,2048]{1,0:T(8,128)} %flat_in.1, s32[2,128,2048]{2,1,0:T(8,128)} %mask_in.1), custom_call_target="tpu_custom_call" | custom-call | tf_op jit(solution)/shard_map/pallas_call | solution.py:537
  55.9 1.9 %copy.9 = f32[1024,128]{1,0:T(8,128)} copy(f32[1024,128]{1,0:T(8,128)} %shard_map.73) | data formatting | bytes 1048576

commit v2 on v1

--- a/solution.py
+++ b/solution.py
@@ -166,7 +166,7 @@
         ref[:, width : 2 * width] = both[band : 2 * band]
 
     if relay:
-        groups = [(0, 0, 1), (1, 0, 1), (0, 1, 3), (1, 1, 3)]
+        groups = [(0, True, 0, 4), (1, True, 0, 4), (0, False, 0, 4), (1, False, 0, 4), (0, False, 4, 12), (1, False, 4, 12)]
 
         def target(index, head):
             group, over = lax.div(index, n_tx), lax.rem(index, n_tx)
@@ -210,7 +210,7 @@
                 copy.start() if start else copy.wait_send()
 
     else:
-        groups = [(expo, 1, n_ty) for expo in range(exposures)]
+        groups = [(expo, False, 0, n_tx * n_ty) for expo in range(exposures)]
 
         def target(index, head):
             group, over = lax.div(index, n_tx), lax.rem(index, n_tx)
@@ -238,14 +238,14 @@
                 copy.start() if start else copy.wait_send()
 
     def over_group(group, *actions):
-        expo, tail, length = group
+        expo, head, first, end = group
 
         def step(index, carry):
             for action in actions:
-                action(expo, index, tail == 0)
+                action(expo, index, head)
             return carry
 
-        lax.fori_loop(0, length * n_tx, step, 0)
+        lax.fori_loop(first, end, step, 0)
 
     def begin(expo, index, head):
         dispatch(expo, index, head, True)
@@ -253,26 +253,29 @@
     def finish_send(expo, index, head):
         dispatch(expo, index, head, False)
 
-    for expo in range(exposures):
-        weigh(expo, 1)
+    def send_stat(step, carry):
+        stat_copy(me, step).start()
+        return carry
+
+    weigh(0, 1)
     loads[0].wait()
     loads[1].wait()
     for expo in range(exposures):
+        if expo > 0:
+            weigh(expo, 1)
         loads[2 + 2 * expo].wait()
         loads[3 + 2 * expo].wait()
         correct(expo)
-    if relay:
-        over_group(groups[0], prepare)
-    pl.semaphore_wait(barrier, parts + visits - 2)
-
-    def send_stat(step, carry):
-        stat_copy(me, step).start()
-        return carry
-
+        if expo == 0:
+            if relay:
+                over_group(groups[0], prepare)
+            pl.semaphore_wait(barrier, parts + visits - 2)
+            if relay:
+                over_group(groups[0], begin)
+    for group in groups[1 if relay else 0 : 2 if relay else 1]:
+        over_group(group, prepare, begin)
     lax.fori_loop(1, parts, send_stat, 0)
-    if relay:
-        over_group(groups[0], begin)
-    for group in groups[1 if relay else 0 :]:
+    for group in groups[2 if relay else 1 :]:
         over_group(group, prepare, begin)
 
     for expo in range(exposures):
@@ -457,18 +460,20 @@
         for step in range(1, visits):
             sum_copy(step, block).wait()
             total = total + partial[step, block_rows(block), :]
-        if relay:
-            totals[pl.ds(pl.multiple_of(vi * own + block * BLOCK, BLOCK), BLOCK), :] = total
-
-            @pl.when(outer)
-            def _():
+        out[block_rows(block), :] = total[:, 0:width] / jnp.maximum(total[:, width : 2 * width], 1.0)
+        return carry
+
+    if relay:
+
+        @pl.when(outer)
+        def _():
+            def receive(block, carry):
                 relay_copy(block).wait_recv()
                 at = pl.ds(pl.multiple_of(vi * own + block * BLOCK, BLOCK), BLOCK)
-                totals[at, :] = total + relay_in[block_rows(block), :].astype(jnp.float32)
-
-            total = totals[pl.ds(pl.multiple_of(vi * own + block * BLOCK, BLOCK), BLOCK), :]
-        out[block_rows(block), :] = total[:, 0:width] / jnp.maximum(total[:, width : 2 * width], 1.0)
-        return carry
+                totals[at, :] = totals[at, :] + relay_in[block_rows(block), :].astype(jnp.float32)
+                return carry
+
+            lax.fori_loop(0, blocks, receive, 0)
 
     lax.fori_loop(0, blocks, finish, 0)
 

time: 57.9 us -> 53 us (0.915)
  Pallas kernels: 55.8 us -> 51 us
    pallas_call x1, Pallas kernels: 55.8 us -> 51 us  [shards(): pl.pallas_call(functools.partial(kernel, dims), out_shape=jax.ShapeDtypeS...]
where the time goes in v2:
time: 53 us; the launch traced here: 52.9 us
  Pallas kernels  51 us (96%)
  local copies, waits for them, and re-layouts  1.87 us (4%)
    pallas_call x1, Pallas kernels, shards(): pl.pallas_call(functools.partial(kernel, dims), out_shape=jax.ShapeDtypeS...  51 us
    unnamed x1, local copies, waits for them, and re-layouts  1.87 us

profile of v2, /device:TPU:0, one launch (start us, length us, event | category | flops | bytes accessed | tf_op | source)
XLA Modules:
  0.0 52.9 jit_solution(15659181172908495454)
XLA Ops:
  0.0 51.0 %shard_map.73 = f32[1024,128]{1,0:T(8,128)} custom-call(s32[2,2]{1,0:T(2,128)} %offsets.1, f32[2,2]{1,0:T(2,128)} %scales.1, f32[2,2]{1,0:T(2,128)} %fracs.1, bf16[2,128,2048]{2,1,0:T(8,128)(2,1)} %raw_in.1, f32[128,2048]{1,0:T(8,128)} %dark_in.1, f32[128,2048]{1,0:T(8,128)} %flat_in.1, s32[2,128,2048]{2,1,0:T(8,128)} %mask_in.1), custom_call_target="tpu_custom_call" | custom-call | tf_op jit(solution)/shard_map/pallas_call | solution.py:542
  51.0 1.9 %copy.9 = f32[1024,128]{1,0:T(8,128)} copy(f32[1024,128]{1,0:T(8,128)} %shard_map.73) | data formatting | bytes 1048576
